TPU v7x, 32 devices: a whole 2x2x4 slice. The times are simulated.
32 devices in a mesh: pair: 8 (over y, x, core), grp: 4 (over z).
Axes of the slice: x: 2, y: 2, z: 4, core: 2. Of those that a mesh axis runs over, the one named last changes fastest.
Arguments:
- amplitudes: float32 [64, 64, 4096], P('pair'), may hold values from -6 to 6
- integrals: float32 [4, 8, 4, 64, 4096], P('grp', 'pair'), may hold values from -0.09375 to 0.09375
- tasks: int32 [4, 8, 4], P('grp', 'pair'), may hold values from -1 to 63, as said below
Outputs:
- residual: float32 [4, 512, 64], P('grp', 'pair')
Inputs may be any that keep to these rules, and one draw needn't show every extreme that they name: `tasks`: in each device's list the live entries (not -1) come first and are distinct; every device has at least one live entry, and in every index of grp some device has all 4 live.
All inputs are finite; a program needn't handle non-finite values.
Results may differ from a plain program's by a relative error of at most 0.0003.
Values sent between devices are 32-bit elements; how exact they have to be, the bound alone decides.
A program may use at most 128 MiB of HBM per device.

v0:
```python
import jax
import jax.numpy as jnp
from jax import lax
from jax.sharding import PartitionSpec as P

NT = 8


def body(amplitudes, integrals, tasks):
    moved = lax.all_to_all(amplitudes, "pair", split_axis=1, concat_axis=0, tiled=True)
    blocks = integrals[0, 0]
    codes = tasks[0, 0]
    slots = codes.shape[0]
    width = blocks.shape[1]
    local_pairs = moved.shape[1]
    pair_rows = moved.shape[0]
    total = jnp.zeros((NT, width, pair_rows), jnp.float32)
    for slot in range(slots):
        block = blocks[slot]
        contribution_code = codes[slot]
        contribution_valid = contribution_code >= 0
        safe = jnp.maximum(contribution_code, 0)
        chosen = lax.dynamic_index_in_dim(moved, safe % local_pairs, 1, keepdims=False)

        def compute():
            return lax.dot_general(
                block,
                chosen,
                (((1,), (1,)), ((), ())),
                precision=lax.Precision.HIGHEST,
                preferred_element_type=jnp.float32,
            )

        def nothing():
            return jnp.zeros((width, pair_rows), jnp.float32)

        code = codes[slot]
        valid = code >= 0
        tile = jnp.maximum(code, 0) // local_pairs
        selector = ((jnp.arange(NT, dtype=jnp.int32) == tile) & valid).astype(jnp.float32)
        total = (
            total
            + selector[:, None, None] * lax.cond(contribution_valid, compute, nothing)[None, :, :]
        )
    partial_value = total.reshape(NT * width, pair_rows)
    summed = lax.psum_scatter(partial_value, "pair", scatter_dimension=0, tiled=True)
    return summed[None]


def solution(mesh):
    return jax.shard_map(
        body,
        mesh=mesh,
        in_specs=(
            P("pair", None, None),
            P("grp", "pair", None, None, None),
            P("grp", "pair", None),
        ),
        out_specs=P("grp", "pair", None),
        check_vma=False,
    )
```

profile of v0, /device:TPU:0, one launch (start us, length us, event | category | flops | bytes accessed | tf_op | source)
XLA Modules:
  0.0 200.6 jit_solution(8746920308982687962)
XLA Ops:
  6.5 11.5 %copy.9 = f32[8,64,4096]{2,0,1:T(8,128)} copy(f32[8,64,4096]{2,1,0:T(8,128)} %param.11) | data formatting | bytes 16777216 | tf_op args[0]
  18.0 5.3 %all-to-all-start = ((f32[8,64,4096]{2,0,1:T(8,128)}), f32[8,64,4096]{2,0,1:T(8,128)}, u32[]{:S(2)}, u32[]{:S(2)}) async-start(f32[8,64,4096]{2,0,1:T(8,128)} %copy.9), calls=%async_computation | async-start | bytes 16777216 | tf_op jit(solution)/shard_map/all_to_all | solution.py:10
  23.3 0.0 reduce-scatter.2.cloned.1.call-start
  23.4 0.7 fusion.19
  29.1 0.1 mul.98
  29.2 0.1 mul.99
  29.3 0.1 mul.92
  29.4 0.1 mul.93
  29.5 0.1 mul.86
  29.5 0.1 mul.87
  29.6 0.1 mul.80
  29.7 0.1 mul.81
  29.8 88.1 %all-to-all-done = f32[8,64,4096]{2,0,1:T(8,128)} async-done(((f32[8,64,4096]{2,0,1:T(8,128)}), f32[8,64,4096]{2,0,1:T(8,128)}, u32[]{:S(2)}, u32[]{:S(2)}) %all-to-all-start) | async-done | bytes 8388640 | tf_op jit(solution)/shard_map/all_to_all | solution.py:10
  117.9 11.6 %copy.10 = f32[8,8,8,4096]{3,2,1,0:T(8,128)} copy(f32[8,8,8,4096]{3,1,2,0:T(8,128)} %bitcast.13) | data formatting | bytes 16777216 | tf_op jit(solution)/shard_map/all_to_all | solution.py:10
  129.5 0.1 copy.14
  129.6 0.1 copy.13
  129.7 0.1 copy.12
  129.8 7.2 %conditional.4 = (f32[64,64]{0,1:T(8,128)S(1)}) conditional(s32[]{:T(128)} %convert_element_type.41, () %tuple.37, (s32[]{:T(128)}, f32[64,8,4096]{2,1,0:T(8,128)}, f32[1,1,4,64,4096]{4,3,2,1,0:T(8,128)}, s32[]{:T(128)}, s32[]{:T(128)}, /*index=5*/pred[]{:T(512)}, s32[]{:T(128)}, s32[]{:T(128)}) %tuple.61), branch_computations={%region_0.1_spmd, %region_1.2_spmd} | conditional | flops 201326592 | bytes 4210771 | solution.py:43
  129.8 4.4 %constant_dynamic-slice_fusion = f32[64,1,4096]{2,1,0:T(1,128)S(1)} fusion(f32[64,8,4096]{2,1,0:T(8,128)} %get-tuple-element.149, s32[]{:T(128)S(6)} %select_n.41), kind=kLoop, calls=%fused_computation.5 | loop fusion | bytes 2097156 | tf_op jit(solution)/shard_map/jit(dynamic_index_in_dim)/dynamic_slice | solution.py:23
  134.2 2.8 %convolution_bitcast_fusion = f32[64,64]{0,1:T(8,128)S(1)} fusion(f32[64,1,4096]{2,1,0:T(1,128)S(1)} %constant_dynamic-slice_fusion, f32[1,1,4,64,4096]{4,3,2,1,0:T(8,128)} %get-tuple-element.151), kind=kOutput, calls=%fused_computation | convolution fusion | flops 201326592 | bytes 2113536 | tf_op jit(solution)/shard_map/cond/branch_1_fun/dot_general | solution.py:26
  137.0 0.1 copy.11
  137.1 1.0 fusion.16
  138.1 0.0 reduce-scatter.2.cloned.1.call-update
  138.1 55.6 %reduce-scatter.2.cloned.1.call-done = f32[64,64]{1,0:T(8,128)} async-done(((f32[512,64]{1,0:T(8,128)}), f32[64,64]{1,0:T(8,128)}) %reduce-scatter.2.cloned.1.call-update) | async-done | bytes 16400 | tf_op jit(solution)/shard_map/reduce_scatter | solution.py:46
  (12 shorter events, 0.1 us)
Async XLA Ops:
  18.0 5.4 %copy-start = (s32[1,1,4]{2,1,0:T(1,128)S(1)}, s32[1,1,4]{2,1,0:T(1,128)}, u32[]{:S(2)}) copy-start(s32[1,1,4]{2,1,0:T(1,128)} %param.13) | copy-start | bytes 52
  18.0 99.9 %all-to-all-start = ((f32[8,64,4096]{2,0,1:T(8,128)}), f32[8,64,4096]{2,0,1:T(8,128)}, u32[]{:S(2)}, u32[]{:S(2)}) async-start(f32[8,64,4096]{2,0,1:T(8,128)} %copy.9), calls=%async_computation | async-start | bytes 16777216 | tf_op jit(solution)/shard_map/all_to_all | solution.py:10
  23.3 170.4 %reduce-scatter.2.cloned.1.call-start = ((), (), s32[]{:S(2)}) async-start(), calls=%async_computation.2 | async-start | bytes 294912 | tf_op jit(solution)/shard_map/reduce_scatter | solution.py:46
Sparse Core Ops, SparseCore 0:
  138.3 55.4 reduce-scatter.1
where the time goes:
time: 201 us
  waiting for transfers between devices  144 us (72%)
  local copies, waits for them, and re-layouts  29.1 us (14%)
  between operations  18.5 us (9%)
  starting transfers between devices  5.37 us (3%)
  matrix products  2.77 us (1%)
    all_to_all x1, waiting for transfers between devices, body(): lax.all_to_all(amplitudes, 'pair', split_axis=1, concat_axis=0, tiled=True)  88.1 us
    reduce_scatter x1, waiting for transfers between devices, body(): lax.psum_scatter(partial_value, 'pair', scatter_dimension=0, tiled=True)  55.6 us
    all_to_all x1, local copies, waits for them, and re-layouts, body(): lax.all_to_all(amplitudes, 'pair', split_axis=1, concat_axis=0, tiled=True)  11.6 us
    unnamed x3, local copies, waits for them, and re-layouts  11.5 us
    all_to_all x1, starting transfers between devices, body(): lax.all_to_all(amplitudes, 'pair', split_axis=1, concat_axis=0, tiled=True)  5.33 us
    dynamic_slice x1, local copies, waits for them, and re-layouts, body(): lax.dynamic_index_in_dim(moved, safe % local_pairs, 1, keepdims=False)  4.44 us
  transfers between devices with their start and end apart: 2, of which 2 were waited for; matrix products, arithmetic and copies ran while one was open for 1% of the time, Pallas kernels for 0%

commit v1 on v0

v1 whole, which is shorter than its diff:
```python
import functools

import jax
import jax.numpy as jnp
from jax import lax
from jax.experimental import pallas as pl
from jax.experimental.pallas import tpu as pltpu
from jax.sharding import PartitionSpec as P

NT = 8
MESH = pl.DeviceIdType.MESH


def split(x):
    high = x.astype(jnp.bfloat16)
    low = (x - high.astype(jnp.float32)).astype(jnp.bfloat16)
    return jnp.concatenate([high, low], axis=0)


def kernel(n, columns, tasks_ref, amp_ref, int_ref, out_ref, listed, amp, blocks, sent, held, total, parts,
           local_sem, list_send, list_recv, send_sem, recv_sem, part_send, part_recv):
    me = lax.axis_index("pair")
    grp = lax.axis_index("grp")
    own_rows, pairs, depth = amp_ref.shape
    slots, width, _ = int_ref.shape
    local = pairs // n
    part_rows = out_ref.shape[0]
    lists = columns < local

    load_amp = pltpu.make_async_copy(amp_ref, amp, local_sem.at[0])
    load_int = pltpu.make_async_copy(int_ref, blocks, local_sem.at[1])
    load_amp.start()
    load_int.start()

    def other(d):
        return lax.rem(me + d, n)

    def target(p):
        return (p, grp)

    barrier = pltpu.get_barrier_semaphore()

    @pl.loop(1, n)
    def _(d):
        pl.semaphore_signal(barrier, inc=1, device_id=target(other(d)), device_id_type=MESH)

    pl.semaphore_wait(barrier, n - 1)

    def list_copy(frm, to):
        return pltpu.make_async_remote_copy(
            src_ref=tasks_ref, dst_ref=listed.at[frm], send_sem=list_send.at[to], recv_sem=list_recv.at[frm],
            device_id=target(to), device_id_type=MESH)

    def column_copy(c, frm, to):
        return pltpu.make_async_remote_copy(
            src_ref=sent.at[c, to], dst_ref=held.at[c, frm], send_sem=send_sem.at[c, to],
            recv_sem=recv_sem.at[c, frm], device_id=target(to), device_id_type=MESH)

    def part_copy(frm, to):
        return pltpu.make_async_remote_copy(
            src_ref=total.at[to], dst_ref=parts.at[frm], send_sem=part_send.at[to],
            recv_sem=part_recv.at[frm], device_id=target(to), device_id_type=MESH)

    if lists:
        @pl.loop(1, n)
        def _(d):
            list_copy(me, other(d)).start()

        @pl.loop(1, n)
        def _(d):
            list_copy(other(d), other(d)).wait_recv()

    load_amp.wait()

    def column(p, c, codes):
        if lists:
            return p * local + lax.rem(jnp.maximum(codes(c), 0), local)
        return p * local + c

    for c in range(columns):
        @pl.loop(1, n)
        def _(d):
            p = other(d)
            at = column(p, c, lambda k: listed[p, 0, k])
            for row in range(own_rows):
                sent[c, p, pl.ds(row, 1), :] = amp[row, pl.ds(at, 1), :]

            @pl.when(d > 1)
            def _():
                column_copy(c, me, other(d - 1)).start()

        at = column(me, c, lambda k: tasks_ref[0, k])
        for row in range(own_rows):
            held[c, me, pl.ds(row, 1), :] = amp[row, pl.ds(at, 1), :]
        column_copy(c, me, other(n - 1)).start()

    load_int.wait()
    total[...] = jnp.zeros_like(total)

    def arrive(c):
        @pl.loop(1, n)
        def _(d):
            column_copy(c, other(d), other(d)).wait_recv()

    if not lists:
        for c in range(columns):
            arrive(c)

    @pl.loop(0, slots)
    def _(slot):
        code = tasks_ref[0, slot]
        safe = jnp.maximum(code, 0)
        if lists:
            arrive(slot)
            chosen = held[slot]
        else:
            chosen = held[lax.rem(safe, local)]
        chosen = chosen.reshape(n * own_rows, depth)
        rows = split(blocks[slot])
        both = lax.dot_general(rows, split(chosen), (((1,), (1,)), ((), ())), preferred_element_type=jnp.float32)
        both = both[:width] + both[width:]
        term = both[:, : n * own_rows] + both[:, n * own_rows:]
        tile = jnp.where(code >= 0, lax.div(safe, local), -1)
        for p in range(n):
            first = p * part_rows
            total[p] += jnp.where(tile == first // width, term[first % width: first % width + part_rows], 0.0)

    @pl.loop(1, n)
    def _(d):
        part_copy(me, other(d)).start()

    parts[me] = total[me]

    @pl.loop(1, n)
    def _(d):
        part_copy(other(d), other(d)).wait_recv()

    result = parts[0]
    for p in range(1, n):
        result += parts[p]
    out_ref[...] = result

    @pl.loop(1, n)
    def _(d):
        part_copy(me, other(d)).wait_send()
        if lists:
            list_copy(me, other(d)).wait_send()
        for c in range(columns):
            column_copy(c, me, other(d)).wait_send()


def body(n, amplitudes, integrals, tasks):
    own_rows, pairs, depth = amplitudes.shape
    slots, width = integrals.shape[2:4]
    local = pairs // n
    columns = min(local, slots)
    part_rows = NT * width // n
    out = pl.pallas_call(
        functools.partial(kernel, n, columns),
        out_shape=jax.ShapeDtypeStruct((part_rows, n * own_rows), jnp.float32),
        in_specs=[
            pl.BlockSpec(memory_space=pltpu.SMEM),
            pl.BlockSpec(memory_space=pl.ANY),
            pl.BlockSpec(memory_space=pl.ANY),
        ],
        out_specs=pl.BlockSpec(memory_space=pltpu.VMEM),
        scratch_shapes=[
            pltpu.SMEM((n, 1, slots), jnp.int32),
            pltpu.VMEM(amplitudes.shape, jnp.float32),
            pltpu.VMEM((slots, width, depth), jnp.float32),
            pltpu.VMEM((columns, n, own_rows, depth), jnp.float32),
            pltpu.VMEM((columns, n, own_rows, depth), jnp.float32),
            pltpu.VMEM((n, part_rows, n * own_rows), jnp.float32),
            pltpu.VMEM((n, part_rows, n * own_rows), jnp.float32),
            pltpu.SemaphoreType.DMA((2,)),
            pltpu.SemaphoreType.DMA((n,)),
            pltpu.SemaphoreType.DMA((n,)),
            pltpu.SemaphoreType.DMA((columns, n)),
            pltpu.SemaphoreType.DMA((columns, n)),
            pltpu.SemaphoreType.DMA((n,)),
            pltpu.SemaphoreType.DMA((n,)),
        ],
        compiler_params=pltpu.CompilerParams(
            collective_id=0, has_side_effects=True, vmem_limit_bytes=60 * 1024 * 1024),
    )(tasks[0], amplitudes, integrals[0, 0])
    return out[None]


def solution(mesh):
    return jax.shard_map(
        functools.partial(body, mesh.shape["pair"]),
        mesh=mesh,
        in_specs=(
            P("pair", None, None),
            P("grp", "pair", None, None, None),
            P("grp", "pair", None),
        ),
        out_specs=P("grp", "pair", None),
        check_vma=False,
    )
```

time: 201 us -> 61.8 us (0.31)
  waiting for transfers between devices: 144 us -> 0 us
  Pallas kernels: 0 us -> 60.2 us
  local copies, waits for them, and re-layouts: 29.1 us -> 1.38 us
  between operations: 18.5 us -> 0.01 us
  starting transfers between devices: 5.37 us -> 0 us
  matrix products: 2.77 us -> 0 us
    all_to_all x1 -> x0, waiting for transfers between devices: 88.1 us -> none  [body(): lax.all_to_all(amplitudes, 'pair', split_axis=1, concat_axis=0, tiled=True)]
    pallas_call x0 -> x1, Pallas kernels: none -> 60.2 us  [body(): pl.pallas_call(functools.partial(kernel, n, columns), out_shape=jax.Shape...]
    reduce_scatter x1 -> x0, waiting for transfers between devices: 55.6 us -> none  [body(): lax.psum_scatter(partial_value, 'pair', scatter_dimension=0, tiled=True)]
    all_to_all x1 -> x0, local copies, waits for them, and re-layouts: 11.6 us -> none  [body(): lax.all_to_all(amplitudes, 'pair', split_axis=1, concat_axis=0, tiled=True)]
    unnamed x3 -> x1, local copies, waits for them, and re-layouts: 11.5 us -> 1.38 us
    all_to_all x1 -> x0, starting transfers between devices: 5.33 us -> none  [body(): lax.all_to_all(amplitudes, 'pair', split_axis=1, concat_axis=0, tiled=True)]
    dynamic_slice x1 -> x0, local copies, waits for them, and re-layouts: 4.44 us -> none  [body(): lax.dynamic_index_in_dim(moved, safe % local_pairs, 1, keepdims=False)]
    dot_general x1 -> x0, matrix products: 2.77 us -> none  [compute(): lax.dot_general(block, chosen, (((1,), (1,)), ((), ())), precision=lax.Pr...]
  transfers between devices with their start and end apart: 2 -> 0, of which waited for: 2 -> 0; matrix products, arithmetic and copies ran while one was open for 1% -> 0% of each run, Pallas kernels for 0% -> 0%
where the time goes in v1:
time: 61.8 us; the launch traced here: 61.6 us
  Pallas kernels  60.2 us (97%)
  local copies, waits for them, and re-layouts  1.38 us (2%)
    pallas_call x1, Pallas kernels, body(): pl.pallas_call(functools.partial(kernel, n, columns), out_shape=jax.Shape...  60.2 us
    unnamed x1, local copies, waits for them, and re-layouts  1.38 us

profile of v1, /device:TPU:0, one launch (start us, length us, event | category | flops | bytes accessed | tf_op | source)
XLA Modules:
  0.0 61.6 jit_solution(4451237646087653298)
XLA Ops:
  0.0 60.2 %shard_map.37 = f32[64,64]{1,0:T(8,128)} custom-call(s32[1,4]{1,0:T(1,128)} %bitcast.5, f32[8,64,4096]{2,1,0:T(8,128)} %amp_ref.1, f32[4,64,4096]{2,1,0:T(8,128)} %bitcast.3), custom_call_target="tpu_custom_call" | custom-call | tf_op jit(solution)/shard_map/pallas_call | solution.py:158
  60.2 1.4 %copy.5 = f32[1,64,64]{2,1,0:T(8,128)} copy(f32[1,64,64]{2,1,0:T(8,128)} %bitcast.4) | data formatting | bytes 32768

commit v2 on v1

v2 whole, which is shorter than its diff:
```python
import functools

import jax
import jax.numpy as jnp
from jax import lax
from jax.experimental import pallas as pl
from jax.experimental.pallas import tpu as pltpu
from jax.sharding import PartitionSpec as P

NT = 8
SHARED = 896
MESH = pl.DeviceIdType.MESH


def split(x):
    high = x.astype(jnp.bfloat16)
    low = (x - high.astype(jnp.float32)).astype(jnp.bfloat16)
    return jnp.concatenate([high, low], axis=0)


def kernel(n, layers, columns, shared, pack, tasks_ref, amp_ref, int_ref, out_ref, listed, amp, blocks, rows, sent,
           held, sent_shared, held_shared, total, parts, local_sem, list_send, list_recv, send_sem, recv_sem,
           fetch_send, fetch_recv, layer_send, layer_recv, part_send, part_recv):
    me = lax.axis_index("pair")
    grp = lax.axis_index("grp")
    own_rows, pairs, depth = amp_ref.shape
    slots, width, _ = int_ref.shape
    local = pairs // n
    per = local // layers if shared else 1
    part_rows = out_ref.shape[0]
    lists = columns < local
    tail = pl.ds(shared, depth - shared)

    load_amp = pltpu.make_async_copy(amp_ref, amp, local_sem.at[0])
    load_int = pltpu.make_async_copy(int_ref, blocks, local_sem.at[1])
    load_amp.start()
    load_int.start()

    def other(d):
        return lax.rem(me + d, n)

    def target(p):
        return (p, grp)

    barrier = pltpu.get_barrier_semaphore()

    @pl.loop(1, n)
    def _(d):
        pl.semaphore_signal(barrier, inc=1, device_id=target(other(d)), device_id_type=MESH)

    if shared:
        @pl.when(grp > 0)
        def _():
            pl.semaphore_signal(barrier, inc=1, device_id=(me, grp - 1), device_id_type=MESH)

        @pl.when(grp < layers - 1)
        def _():
            pl.semaphore_signal(barrier, inc=1, device_id=(me, grp + 1), device_id_type=MESH)

        peers = n - 1 + jnp.minimum(grp, 1) + jnp.minimum(layers - 1 - grp, 1)
        pl.semaphore_wait(barrier, peers)
    else:
        pl.semaphore_wait(barrier, n - 1)

    def list_copy(frm, to):
        return pltpu.make_async_remote_copy(
            src_ref=tasks_ref, dst_ref=listed.at[frm], send_sem=list_send.at[to], recv_sem=list_recv.at[frm],
            device_id=target(to), device_id_type=MESH)

    def column_copy(c, frm, to):
        return pltpu.make_async_remote_copy(
            src_ref=sent.at[c, to], dst_ref=held.at[c, frm], send_sem=send_sem.at[c, to],
            recv_sem=recv_sem.at[c, frm], device_id=target(to), device_id_type=MESH)

    def fetch_copy(j, frm, to):
        return pltpu.make_async_remote_copy(
            src_ref=sent_shared.at[j, to], dst_ref=held_shared.at[grp * per + j, frm],
            send_sem=fetch_send.at[j, to], recv_sem=fetch_recv.at[j, frm], device_id=target(to), device_id_type=MESH)

    def layer_copy(block, j, step):
        at = held_shared.at[block * per + j]
        return pltpu.make_async_remote_copy(
            src_ref=at, dst_ref=at, send_sem=layer_send.at[(step + 1) // 2, block * per + j],
            recv_sem=layer_recv.at[block * per + j], device_id=(me, grp + step), device_id_type=MESH)

    def part_copy(frm, to):
        return pltpu.make_async_remote_copy(
            src_ref=total.at[to], dst_ref=parts.at[frm], send_sem=part_send.at[to],
            recv_sem=part_recv.at[frm], device_id=target(to), device_id_type=MESH)

    if lists:
        @pl.loop(1, n)
        def _(d):
            list_copy(me, other(d)).start()

    load_amp.wait()

    if shared:
        for j in range(per):
            @pl.loop(1, n)
            def _(d):
                p = other(d)
                for row in range(own_rows):
                    sent_shared[j, p, pl.ds(row, 1), :] = amp[
                        row, pl.ds(p * local + grp * per + j, 1), pl.ds(0, shared)]

                @pl.when(d > 1)
                def _():
                    fetch_copy(j, me, other(d - 1)).start()

            for row in range(own_rows):
                held_shared[grp * per + j, me, pl.ds(row, 1), :] = amp[
                    row, pl.ds(me * local + grp * per + j, 1), pl.ds(0, shared)]
            fetch_copy(j, me, other(n - 1)).start()

    if lists:
        @pl.loop(1, n)
        def _(d):
            list_copy(other(d), other(d)).wait_recv()

    def column(p, c, codes):
        if lists:
            return p * local + lax.rem(jnp.maximum(codes(c), 0), local)
        return p * local + c

    for c in range(columns):
        @pl.loop(1, n)
        def _(d):
            p = other(d)
            at = column(p, c, lambda k: listed[p, 0, k])
            for row in range(own_rows):
                sent[c, p, pl.ds(row, 1), :] = amp[row, pl.ds(at, 1), tail]

            @pl.when(d > 1)
            def _():
                column_copy(c, me, other(d - 1)).start()

        at = column(me, c, lambda k: tasks_ref[0, k])
        for row in range(own_rows):
            held[c, me, pl.ds(row, 1), :] = amp[row, pl.ds(at, 1), tail]
        column_copy(c, me, other(n - 1)).start()

    def forward(hop, j, act):
        @pl.when((grp - hop >= 0) & (grp + 1 < layers))
        def _():
            act(layer_copy(grp - hop, j, 1))

        @pl.when((grp + hop < layers) & (grp >= 1))
        def _():
            act(layer_copy(grp + hop, j, -1))

    def stage(hop):
        for j in range(per):
            @pl.when(grp - hop >= 0)
            def _():
                layer_copy(grp - hop, j, 1).wait_recv()

            @pl.when(grp + hop < layers)
            def _():
                layer_copy(grp + hop, j, -1).wait_recv()

            if hop < layers - 1:
                forward(hop, j, lambda copy: copy.start())

    load_int.wait()

    @pl.loop(0, slots)
    def _(slot):
        rows[slot] = split(blocks[slot])

    total[...] = jnp.zeros_like(total)

    if shared:
        for j in range(per):
            @pl.loop(1, n)
            def _(d):
                fetch_copy(j, other(d), other(d)).wait_recv()

            forward(0, j, lambda copy: copy.start())

    def arrive(c):
        @pl.loop(1, n)
        def _(d):
            column_copy(c, other(d), other(d)).wait_recv()

    def add(slot, chosen, span):
        code = tasks_ref[0, slot]
        chosen = chosen.reshape(n * own_rows, chosen.shape[-1])
        both = lax.dot_general(rows[slot, :, span], split(chosen), (((1,), (1,)), ((), ())),
                               preferred_element_type=jnp.float32)
        both = both[:width] + both[width:]
        term = both[:, : n * own_rows] + both[:, n * own_rows:]
        tile = jnp.where(code >= 0, lax.div(jnp.maximum(code, 0), local), -1)
        piece = part_rows // pack
        packed = {}
        for p in range(n):
            first = p * part_rows
            low = first % width
            if low not in packed:
                packed[low] = jnp.concatenate(
                    [term[low + i * piece: low + (i + 1) * piece] for i in range(pack)], axis=1)
            total[p] += jnp.where(tile == first // width, packed[low], 0.0)

    def picked(slot):
        return lax.rem(jnp.maximum(tasks_ref[0, slot], 0), local)

    if lists:
        for slot in range(slots):
            if shared:
                for hop in range(slot + 1, layers if slot == slots - 1 else min(slot + 2, layers)):
                    stage(hop)
            if shared and slot == slots - 1:
                @pl.loop(0, slots)
                def _(each):
                    add(each, held_shared[picked(each)], pl.ds(0, shared))

            arrive(slot)
            add(slot, held[slot], tail)
    else:
        for c in range(columns):
            arrive(c)

        @pl.loop(0, slots)
        def _(slot):
            add(slot, held[picked(slot)], tail)

    @pl.loop(1, n)
    def _(d):
        part_copy(me, other(d)).start()

    parts[me] = total[me]

    @pl.loop(1, n)
    def _(d):
        part_copy(other(d), other(d)).wait_recv()

    result = parts[0]
    for p in range(1, n):
        result += parts[p]
    piece = part_rows // pack
    for i in range(pack):
        out_ref[i * piece: (i + 1) * piece, :] = result[:, i * n * own_rows: (i + 1) * n * own_rows]

    if shared:
        for hop in range(layers - 1):
            for j in range(per):
                forward(hop, j, lambda copy: copy.wait_send())

    @pl.loop(1, n)
    def _(d):
        part_copy(me, other(d)).wait_send()
        if lists:
            list_copy(me, other(d)).wait_send()
        if shared:
            for j in range(per):
                fetch_copy(j, me, other(d)).wait_send()
        for c in range(columns):
            column_copy(c, me, other(d)).wait_send()


def body(n, layers, amplitudes, integrals, tasks):
    own_rows, pairs, depth = amplitudes.shape
    slots, width = integrals.shape[2:4]
    local = pairs // n
    columns = min(local, slots)
    part_rows = NT * width // n
    held_rows = n * own_rows
    pack = max(1, 128 // held_rows)
    shared = SHARED if columns < local and local % layers == 0 else 0
    per = local // layers if shared else 1
    span = max(shared, 128)
    heads = n if shared else 1
    out = pl.pallas_call(
        functools.partial(kernel, n, layers, columns, shared, pack),
        out_shape=jax.ShapeDtypeStruct((part_rows, held_rows), jnp.float32),
        in_specs=[
            pl.BlockSpec(memory_space=pltpu.SMEM),
            pl.BlockSpec(memory_space=pl.ANY),
            pl.BlockSpec(memory_space=pl.ANY),
        ],
        out_specs=pl.BlockSpec(memory_space=pltpu.VMEM),
        scratch_shapes=[
            pltpu.SMEM((n, 1, slots), jnp.int32),
            pltpu.VMEM(amplitudes.shape, jnp.float32),
            pltpu.VMEM((slots, width, depth), jnp.float32),
            pltpu.VMEM((slots, 2 * width, depth), jnp.bfloat16),
            pltpu.VMEM((columns, n, own_rows, depth - shared), jnp.float32),
            pltpu.VMEM((columns, n, own_rows, depth - shared), jnp.float32),
            pltpu.VMEM((per, heads, own_rows, span), jnp.float32),
            pltpu.VMEM((local, heads, own_rows, span), jnp.float32),
            pltpu.VMEM((n, part_rows // pack, held_rows * pack), jnp.float32),
            pltpu.VMEM((n, part_rows // pack, held_rows * pack), jnp.float32),
            pltpu.SemaphoreType.DMA((2,)),
            pltpu.SemaphoreType.DMA((n,)),
            pltpu.SemaphoreType.DMA((n,)),
            pltpu.SemaphoreType.DMA((columns, n)),
            pltpu.SemaphoreType.DMA((columns, n)),
            pltpu.SemaphoreType.DMA((per, n)),
            pltpu.SemaphoreType.DMA((per, n)),
            pltpu.SemaphoreType.DMA((2, local)),
            pltpu.SemaphoreType.DMA((local,)),
            pltpu.SemaphoreType.DMA((n,)),
            pltpu.SemaphoreType.DMA((n,)),
        ],
        compiler_params=pltpu.CompilerParams(
            collective_id=0, has_side_effects=True, vmem_limit_bytes=60 * 1024 * 1024),
    )(tasks[0], amplitudes, integrals[0, 0])
    return out[None]


def solution(mesh):
    return jax.shard_map(
        functools.partial(body, mesh.shape["pair"], mesh.shape["grp"]),
        mesh=mesh,
        in_specs=(
            P("pair", None, None),
            P("grp", "pair", None, None, None),
            P("grp", "pair", None),
        ),
        out_specs=P("grp", "pair", None),
        check_vma=False,
    )
```

time: 61.8 us -> 55.2 us (0.89)
  Pallas kernels: 60.2 us -> 53.6 us
    pallas_call x1, Pallas kernels: 60.2 us -> 53.6 us  [body(): pl.pallas_call(functools.partial(kernel, n, layers, columns, shared, pack...]
where the time goes in v2:
time: 55.2 us; the launch traced here: 55 us
  Pallas kernels  53.6 us (97%)
  local copies, waits for them, and re-layouts  1.38 us (2%)
    pallas_call x1, Pallas kernels, body(): pl.pallas_call(functools.partial(kernel, n, layers, columns, shared, pack...  53.6 us
    unnamed x1, local copies, waits for them, and re-layouts  1.38 us

profile of v2, /device:TPU:0, one launch (start us, length us, event | category | flops | bytes accessed | tf_op | source)
XLA Modules:
  0.0 55.0 jit_solution(4521935584654619357)
XLA Ops:
  0.0 53.6 %shard_map.37 = f32[64,64]{1,0:T(8,128)} custom-call(s32[1,4]{1,0:T(1,128)} %bitcast.5, f32[8,64,4096]{2,1,0:T(8,128)} %amp_ref.1, f32[4,64,4096]{2,1,0:T(8,128)} %bitcast.3), custom_call_target="tpu_custom_call" | custom-call | tf_op jit(solution)/shard_map/pallas_call | solution.py:273
  53.7 1.4 %copy.5 = f32[1,64,64]{2,1,0:T(8,128)} copy(f32[1,64,64]{2,1,0:T(8,128)} %bitcast.4) | data formatting | bytes 32768
